TPU v7x, 32 devices: a whole 2x2x4 slice. The times are simulated.
32 devices in a mesh: fsdp: 8 (over y, x, core), tensor: 4 (over z).
Axes of the slice: x: 2, y: 2, z: 4, core: 2. Of those that a mesh axis runs over, the one named last changes fastest.
Arguments:
- hidden: bfloat16 [4096, 2048], P(('fsdp', 'tensor')), may hold values from -6 to 6
- cotangent: bfloat16 [4096, 2048], P(('fsdp', 'tensor')), may hold values from -6 to 6
- seq_lengths: int32 [8, 3], P('fsdp'), may hold values from 1 to 256, 512 in all within a row
- pack_order: int32 [8, 3], P('fsdp'), may hold values from 0 to 2, each once within a row
- norm_gain: bfloat16 [2048], P(('fsdp', 'tensor')), may hold values from 0.099609375 to 1.8984375
- w_in: bfloat16 [2, 4096, 2048], P(None, ('fsdp', 'tensor')), may hold values from -0.125 to 0.125
- conv_weight: bfloat16 [4096, 4], P(('fsdp', 'tensor')), may hold values from -3 to 3
- conv_bias: bfloat16 [4096], P(('fsdp', 'tensor')), may hold values from -3 to 3
- w_xproj: bfloat16 [4096, 160], P(('fsdp', 'tensor')), may hold values from -0.1875 to 0.1875
- w_dt: bfloat16 [4096, 128], P(('fsdp', 'tensor')), may hold values from -0.5 to 0.5
- dt_bias: bfloat16 [4096], P(('fsdp', 'tensor')), may hold values from -7 to -2
- a_log: bfloat16 [4096, 16], P(('fsdp', 'tensor')), may hold values from -1 to 2.6875
- d_skip: bfloat16 [4096], P(('fsdp', 'tensor')), may hold values from 0.099609375 to 1.8984375
- w_out: bfloat16 [4096, 2048], P(('fsdp', 'tensor')), may hold values from -0.1875 to 0.1875
Outputs:
- output: bfloat16 [4096, 2048], P(('fsdp', 'tensor'))
- grad_hidden: float32 [4096, 2048], P(('fsdp', 'tensor'))
- grad_norm_gain: float32 [2048], P(('fsdp', 'tensor'))
- grad_w_in: float32 [2, 4096, 2048], P(None, ('fsdp', 'tensor'))
- grad_conv_weight: float32 [4096, 4], P(('fsdp', 'tensor'))
- grad_conv_bias: float32 [4096], P(('fsdp', 'tensor'))
- grad_w_xproj: float32 [4096, 160], P(('fsdp', 'tensor'))
- grad_w_dt: float32 [4096, 128], P(('fsdp', 'tensor'))
- grad_dt_bias: float32 [4096], P(('fsdp', 'tensor'))
- grad_a_log: float32 [4096, 16], P(('fsdp', 'tensor'))
- grad_d_skip: float32 [4096], P(('fsdp', 'tensor'))
- grad_w_out: float32 [4096, 2048], P(('fsdp', 'tensor'))
Inputs may be any that keep to these rules, and one draw needn't show every extreme that they name: `seq_lengths`: each row holds the lengths of the 3 sequences of one token group; they sum to 512 and the largest of each row is exactly 256. `pack_order`: each row is a permutation of 0 to 2: the sequence packed into each slot.
All inputs are finite; a program needn't handle non-finite values.
Results may differ from a plain program's by a relative error of at most 0.012.
Values may be sent and summed in bfloat16 or wider, within the bound.
No kernel may reach another device: no remote copies, remote signals or barrier semaphores. Data moves between devices by JAX's collectives and lax.ppermute only.
A program may use at most 320 MiB of HBM per device.

v0:
```python
import math
import jax
import jax.numpy as jnp
from jax import lax
from jax.sharding import PartitionSpec as P

EPSILON = 1e-05


def normalize(values, scales):
    factor = lax.rsqrt(jnp.mean(values * values, axis=1, keepdims=True) + EPSILON)
    return values * factor * scales[None, :]


def distances(lengths, pack_rows, row_count):
    slot_count = lengths.shape[0]
    picks = pack_rows[:, None] == jnp.arange(slot_count, dtype=jnp.int32)[None, :]
    packed = jnp.sum(jnp.where(picks, lengths[None, :], 0), axis=1)
    starts = jnp.cumsum(packed) - packed
    positions = jnp.arange(row_count, dtype=jnp.int32)
    latest = jnp.max(jnp.where(starts[None, :] <= positions[:, None], starts[None, :], 0), axis=1)
    return positions - latest


def convolve(signal, weights, biases, offsets):
    kernel_taps = weights.shape[1]
    result = biases[None, :] + weights[:, kernel_taps - 1][None, :] * signal
    for lag_index in range(1, kernel_taps):
        shifted = jnp.concatenate(
            [jnp.zeros((lag_index, signal.shape[1]), jnp.float32), signal[:-lag_index]], axis=0
        )
        in_sequence = (offsets >= lag_index).astype(jnp.float32)[:, None]
        result = result + weights[:, kernel_taps - 1 - lag_index][None, :] * shifted * in_sequence
    return result


def block_scan(carried, step_sizes, inputs, b_in, c_out, decays, keep_mask):
    row_count = step_sizes.shape[0]
    stretch_len = math.gcd(row_count, 16)
    stretches = row_count // stretch_len
    channels = step_sizes.shape[1]
    state_cols = decays.shape[1]
    factors = jnp.exp(step_sizes[:, :, None] * decays[None, :, :]) * keep_mask[:, None, None]
    drives = (step_sizes * inputs)[:, :, None] * b_in[:, None, :]
    factors = factors.reshape(stretches, stretch_len, channels, state_cols)
    drives = drives.reshape(stretches, stretch_len, channels, state_cols)
    running = drives[:, 0]
    product = factors[:, 0]
    running_list = [running]
    product_list = [product]
    for offset in range(1, stretch_len):
        running = factors[:, offset] * running + drives[:, offset]
        product = factors[:, offset] * product
        running_list.append(running)
        product_list.append(product)
    running_all = jnp.stack(running_list, axis=1)
    product_all = jnp.stack(product_list, axis=1)

    def carry_step(current, members):
        return (members[0] * current + members[1], current)

    closing, entering = lax.scan(carry_step, carried, (product_all[:, -1], running_all[:, -1]))
    states = running_all + product_all * entering[:, None]
    states = states.reshape(row_count, channels, state_cols)
    return (closing, jnp.sum(states * c_out[:, None, :], axis=2))


def selective(step_sizes, inputs, b_in, c_out, decays, keep_mask, block_len):
    row_count = step_sizes.shape[0]
    blocks = row_count // block_len

    def block_step(carried, pieces):
        return block_scan(carried, pieces[0], pieces[1], pieces[2], pieces[3], decays, pieces[4])

    pieces = (
        step_sizes.reshape(blocks, block_len, -1),
        inputs.reshape(blocks, block_len, -1),
        b_in.reshape(blocks, block_len, -1),
        c_out.reshape(blocks, block_len, -1),
        keep_mask.reshape(blocks, block_len),
    )
    initial = jnp.zeros((step_sizes.shape[1], decays.shape[1]), jnp.float32)
    _, outputs = lax.scan(jax.checkpoint(block_step), initial, pieces)
    return outputs.reshape(row_count, -1)


def mix_states(
    proj, b_in, c_out, inner, gate_in, step_bias, log_rates, skip_scale, keep_mask, block_len
):
    step_sizes = jax.nn.softplus(proj + step_bias[None, :])
    decays = -jnp.exp(log_rates)
    scanned = selective(step_sizes, inner, b_in, c_out, decays, keep_mask, block_len)
    return (scanned + skip_scale[None, :] * inner) * jax.nn.silu(gate_in)


def shards(
    hidden,
    cotangent,
    seq_lengths,
    pack_order,
    norm_gain,
    w_in,
    conv_weight,
    conv_bias,
    w_xproj,
    w_dt,
    dt_bias,
    a_log,
    d_skip,
    w_out,
):
    f32 = jnp.float32
    bf16 = jnp.bfloat16
    n_fsdp = lax.axis_size("fsdp")
    n_tensor = lax.axis_size("tensor")
    tok_rows = hidden.shape[0]
    group_rows = tok_rows * n_tensor
    rank_cols = w_dt.shape[1]
    state_cols = a_log.shape[1]
    block_len = math.gcd(group_rows, 256)
    gathered = (
        lax.all_gather(w_in, "fsdp", axis=1, tiled=True),
        lax.all_gather(conv_weight, "fsdp", axis=0, tiled=True),
        lax.all_gather(conv_bias, "fsdp", axis=0, tiled=True),
        lax.all_gather(w_xproj, "fsdp", axis=0, tiled=True),
        lax.all_gather(w_dt, "fsdp", axis=0, tiled=True),
        lax.all_gather(dt_bias, "fsdp", axis=0, tiled=True),
        lax.all_gather(a_log, "fsdp", axis=0, tiled=True),
        lax.all_gather(d_skip, "fsdp", axis=0, tiled=True),
        lax.all_gather(w_out, "fsdp", axis=0, tiled=True),
        lax.all_gather(norm_gain, "fsdp", axis=0, tiled=True),
    )
    w_in_t, conv_w_t, conv_b_t, w_x_t, w_dt_t, dt_b_t, a_log_t, d_skip_t, w_out_t, gain_fsdp = (
        gathered
    )
    rows_all, gain_tensor = (
        lax.all_gather(hidden, "tensor", axis=0, tiled=True),
        lax.all_gather(gain_fsdp, "tensor", axis=0, tiled=True),
    )
    gain_full = gain_tensor.reshape(n_tensor, n_fsdp, -1).transpose(1, 0, 2).reshape(-1).astype(f32)
    offsets = distances(seq_lengths[0], pack_order[0], group_rows)
    keep_mask = (offsets > 0).astype(f32)
    row_values = rows_all.astype(f32)
    normed = normalize(row_values, gain_full).astype(bf16)
    xz_all = jnp.einsum("gd,hcd->ghc", normed, w_in_t, preferred_element_type=f32)
    signal = xz_all[:, 0]
    gate_in = xz_all[:, 1]
    inner, front_back = jax.vjp(
        lambda signal_in, taps_in, biases_in: jax.nn.silu(
            convolve(signal_in, taps_in, biases_in, offsets)
        ),
        signal,
        conv_w_t.astype(f32),
        conv_b_t.astype(f32),
    )
    inner_low = inner.astype(bf16)
    pieces_x = jnp.dot(inner_low, w_x_t, preferred_element_type=f32)
    mixed = lax.psum(pieces_x, "tensor")
    step_in = mixed[:, :rank_cols].astype(bf16)
    b_in = mixed[:, rank_cols : rank_cols + state_cols]
    c_out = mixed[:, rank_cols + state_cols :]
    proj = jnp.einsum("gr,cr->gc", step_in, w_dt_t, preferred_element_type=f32)
    gated, mixer_back = jax.vjp(
        lambda proj_in, b_part, c_part, inner_in, gate_part, bias_part, rates_part, skip_part: mix_states(
            proj_in,
            b_part,
            c_part,
            inner_in,
            gate_part,
            bias_part,
            rates_part,
            skip_part,
            keep_mask,
            block_len,
        ),
        proj,
        b_in,
        c_out,
        inner_low.astype(f32),
        gate_in,
        dt_b_t.astype(f32),
        a_log_t.astype(f32),
        d_skip_t.astype(f32),
    )
    gated_low = gated.astype(bf16)
    branch = lax.psum_scatter(
        jnp.dot(gated_low, w_out_t, preferred_element_type=f32),
        "tensor",
        scatter_dimension=0,
        tiled=True,
    )
    output = (hidden.astype(f32) + branch).astype(bf16)
    cot_all = lax.all_gather(cotangent, "tensor", axis=0, tiled=True)
    grad_gated = (
        jnp.einsum("gd,cd->gc", cot_all, w_out_t, preferred_element_type=f32)
        .astype(bf16)
        .astype(f32)
    )
    out_grad = jnp.einsum("gc,gd->cd", gated_low, cot_all, preferred_element_type=f32)
    g_proj, g_b, g_c, g_inner_scan, g_gate, g_dt_bias, g_a_log, g_d_skip = mixer_back(grad_gated)
    g_proj_low = g_proj.astype(bf16)
    g_step = jnp.dot(g_proj_low, w_dt_t, preferred_element_type=f32)
    w_dt_grad = jnp.einsum("gc,gr->cr", g_proj_low, step_in, preferred_element_type=f32)
    mixed_grad = lax.psum(jnp.concatenate([g_step, g_b, g_c], axis=1), "tensor")
    mixed_low = mixed_grad.astype(bf16)
    g_inner = g_inner_scan + jnp.einsum("gk,ck->gc", mixed_low, w_x_t, preferred_element_type=f32)
    w_x_grad = jnp.einsum("gc,gk->ck", inner_low, mixed_low, preferred_element_type=f32)
    g_signal, g_conv_w, g_conv_b = front_back(g_inner)
    g_xz = jnp.stack([g_signal, g_gate], axis=1).astype(bf16)
    w_in_grad = jnp.einsum("ghc,gd->hcd", g_xz, normed, preferred_element_type=f32)
    g_normed = jnp.einsum("ghc,hcd->gd", g_xz, w_in_t, preferred_element_type=f32)
    gain_term = jax.vjp(lambda scales: normalize(row_values, scales), gain_full)[1](g_normed)[0]
    gain_term = gain_term.reshape(n_fsdp, n_tensor, -1).transpose(1, 0, 2).reshape(-1)
    g_norm_own, gain_part = (
        lax.psum_scatter(g_normed, "tensor", scatter_dimension=0, tiled=True),
        lax.psum_scatter(gain_term, "tensor", scatter_dimension=0, tiled=True),
    )
    norm_back = jax.vjp(lambda own_values: normalize(own_values, gain_full), hidden.astype(f32))[1]
    grad_hidden = cotangent.astype(f32) + norm_back(g_norm_own)[0]
    results = (
        lax.psum_scatter(w_in_grad, "fsdp", scatter_dimension=1, tiled=True),
        lax.psum_scatter(g_conv_w, "fsdp", scatter_dimension=0, tiled=True),
        lax.psum_scatter(g_conv_b, "fsdp", scatter_dimension=0, tiled=True),
        lax.psum_scatter(w_x_grad, "fsdp", scatter_dimension=0, tiled=True),
        lax.psum_scatter(w_dt_grad, "fsdp", scatter_dimension=0, tiled=True),
        lax.psum_scatter(g_dt_bias, "fsdp", scatter_dimension=0, tiled=True),
        lax.psum_scatter(g_a_log, "fsdp", scatter_dimension=0, tiled=True),
        lax.psum_scatter(g_d_skip, "fsdp", scatter_dimension=0, tiled=True),
        lax.psum_scatter(out_grad, "fsdp", scatter_dimension=0, tiled=True),
        lax.psum_scatter(gain_part, "fsdp", scatter_dimension=0, tiled=True),
    )
    return (
        output,
        grad_hidden,
        results[9],
        results[0],
        results[1],
        results[2],
        results[3],
        results[4],
        results[5],
        results[6],
        results[7],
        results[8],
    )


def solution(mesh):
    placed = (
        P(("fsdp", "tensor"), None),
        P(("fsdp", "tensor"), None),
        P("fsdp", None),
        P("fsdp", None),
        P(("fsdp", "tensor")),
        P(None, ("fsdp", "tensor"), None),
        P(("fsdp", "tensor"), None),
        P(("fsdp", "tensor")),
        P(("fsdp", "tensor"), None),
        P(("fsdp", "tensor"), None),
        P(("fsdp", "tensor")),
        P(("fsdp", "tensor"), None),
        P(("fsdp", "tensor")),
        P(("fsdp", "tensor"), None),
    )
    return jax.shard_map(
        shards,
        mesh=mesh,
        in_specs=placed,
        out_specs=(
            P(("fsdp", "tensor"), None),
            P(("fsdp", "tensor"), None),
            P(("fsdp", "tensor")),
            P(None, ("fsdp", "tensor"), None),
            P(("fsdp", "tensor"), None),
            P(("fsdp", "tensor")),
            P(("fsdp", "tensor"), None),
            P(("fsdp", "tensor"), None),
            P(("fsdp", "tensor")),
            P(("fsdp", "tensor"), None),
            P(("fsdp", "tensor")),
            P(("fsdp", "tensor"), None),
        ),
        check_vma=False,
    )
```

profile of v0, /device:TPU:0, one launch (start us, length us, event | category | flops | bytes accessed | tf_op | source)
XLA Modules:
  0.0 1662.1 jit_solution(14647917128028557112)
XLA Ops:
  12.9 15.5 all-reduce.59
  70.0 43.4 %all-gather.11.cloned.1.call-done = bf16[2,1024,2048]{2,1,0:T(8,128)(2,1)} async-done(((bf16[2,128,2048]{2,1,0:T(8,128)(2,1)}), bf16[2,1024,2048]{2,1,0:T(8,128)(2,1)}) %all-gather.11.cloned.1.call-update) | async-done | bytes 8388624 | tf_op jit(solution)/shard_map/all_gather | solution.py:122
  125.2 35.7 %all-gather.15.cloned.1.call-done = bf16[512,2048]{1,0:T(8,128)(2,1)} async-done(((bf16[128,2048]{1,0:T(8,128)(2,1)}), bf16[512,2048]{1,0:T(8,128)(2,1)}) %all-gather.15.cloned.1.call-update) | async-done | bytes 2097168 | tf_op jit(solution)/shard_map/all_gather | solution.py:193
  160.9 37.2 %all-gather.13.cloned.1.call-done = bf16[1024,2048]{1,0:T(8,128)(2,1)} async-done(((bf16[128,2048]{1,0:T(8,128)(2,1)}), bf16[1024,2048]{1,0:T(8,128)(2,1)}) %all-gather.13.cloned.1.call-update) | async-done | bytes 4194320 | tf_op jit(solution)/shard_map/all_gather | solution.py:130
  255.4 242.1 %while.116 = (s32[]{:T(128)}, f32[1024,16]{0,1:T(8,128)S(1)}, f32[2,256,1024]{2,1,0:T(8,128)}, f32[2,1024,16]{1,2,0:T(8,128)}, f32[2,256,1024]{2,1,0:T(8,128)}, ...) while((s32[]{:T(128)}, f32[1024,16]{0,1:T(8,128)S(1)}, ...), condition=%wide.region_9.10_spmd, body=%wide.region_5.9_spmd.sunk | while | flops 52199424 | bytes 568369280 | solution.py:83
  342.7 24.7 %while.120 = (s32[]{:T(128)}, f32[1024,16]{0,1:T(8,128)S(1)}, f32[16,1024,16]{1,2,0:T(8,128)}, f32[16,1024,16]{1,2,0:T(8,128)}, f32[16,1024,16]{1,2,0:T(8,128)}, /*index=5*/s32[]{:T(128)}) while((s32[]{:T(128)}, f32[1024,16]{0,1:T(8,128)S(1)}, f32[16,1024,16]{1,2,0:T(8,128)}, f32[16,1024,16]{1,2,0:T(8,128)}, f32[16,1024,16]{1,2,0:T(8,128)}, ...), condition=%wide.region_7.7_spmd, body=%wide.region_6.6_spmd.sunk | while | flops 32770 | bytes 393801 | solution.py:62
  457.0 24.7 %while.120 = (s32[]{:T(128)}, f32[1024,16]{0,1:T(8,128)S(1)}, f32[16,1024,16]{1,2,0:T(8,128)}, f32[16,1024,16]{1,2,0:T(8,128)}, f32[16,1024,16]{1,2,0:T(8,128)}, /*index=5*/s32[]{:T(128)}) while((s32[]{:T(128)}, f32[1024,16]{0,1:T(8,128)S(1)}, f32[16,1024,16]{1,2,0:T(8,128)}, f32[16,1024,16]{1,2,0:T(8,128)}, f32[16,1024,16]{1,2,0:T(8,128)}, ...), condition=%wide.region_7.7_spmd, body=%wide.region_6.6_spmd.sunk | while | flops 32770 | bytes 393801 | solution.py:62
  502.0 609.0 %while.119 = (s32[]{:T(128)}, f32[1024,16]{0,1:T(8,128)}, f32[1024,16]{0,1:T(8,128)S(1)}, f32[2,256,1024]{2,1,0:T(8,128)}, f32[2,256,1024]{2,1,0:T(8,128)}, /*in...) while((s32[]{:T(128)}, f32[1024,16]{0,1:T(8,128)}, ...), condition=%wide.region_22.23_spmd.clone, body=%wide.region_11.22_spmd.clone.sunk | while | flops 338518016 | bytes 1045472448 | solution.py:83
  634.5 15.0 while.121
  666.1 24.8 %while.122 = (s32[]{:T(128)}, f32[1024,16]{0,1:T(8,128)S(1)}, f32[16,1024,16]{1,2,0:T(8,128)S(1)}, f32[16,1024,16]{1,2,0:T(8,128)}, f32[16,1024,16]{1,2,0:T(8,12...) while((s32[]{:T(128)}, f32[1024,16]{0,1:T(8,128)S(1)}, ...), condition=%wide.region_16.16_spmd, body=%wide.region_15.15_spmd.sunk | while | flops 49155 | bytes 524401 | solution.py:62
  705.7 15.5 slice_add_fusion.81
  793.8 14.9 multiply_reduce_fusion.17
  923.5 15.0 while.121
  955.2 24.8 %while.122 = (s32[]{:T(128)}, f32[1024,16]{0,1:T(8,128)S(1)}, f32[16,1024,16]{1,2,0:T(8,128)S(1)}, f32[16,1024,16]{1,2,0:T(8,128)}, f32[16,1024,16]{1,2,0:T(8,12...) while((s32[]{:T(128)}, f32[1024,16]{0,1:T(8,128)S(1)}, ...), condition=%wide.region_16.16_spmd, body=%wide.region_15.15_spmd.sunk | while | flops 49155 | bytes 524401 | solution.py:62
  994.8 15.5 slice_add_fusion.81
  1118.0 25.8 %all-reduce.70 = bf16[512,160]{0,1:T(8,128)(2,1)S(1)} all-reduce(f32[512,160]{0,1:T(8,128)S(1)} %pad_maximum_fusion.3), channel_id=1, replica_groups=mesh['fsdp'=8,'tensor'=4] {'tensor'}, use_global_device_ids=true, to_apply=%region_23.24 | all-reduce | flops 81920 | bytes 491520 | tf_op jit(solution)/shard_map/psum | solution.py:204
  1209.2 24.0 %all-reduce.65 = (f32[512]{0:T(512)S(1)}, f32[1024]{0:T(1024)S(1)}, f32[1024]{0:T(1024)S(1)}, f32[1024]{0:T(1024)S(1)}) all-reduce(f32[512]{0:T(512)S(1)} %dynamic-slice.2, f32[1024]{0:T(1024)S(1)} %get-tuple-element.866, f32[1024]{0:T(1024)S(1)} %get-tuple-element.1057, ...), channel_id=5, replica_groups=mesh['fsdp'=8,'tensor'=4] {'fsdp'}, use_global_device_ids=true, to_apply=%region_29.30.clone | all-reduce | flops 3584 | bytes 28672
  1236.9 31.1 %reduce-scatter.13.cloned.1.call-done = f32[128,2048]{1,0:T(8,128)} async-done(((f32[512,2048]{1,0:T(8,128)}), f32[128,2048]{1,0:T(8,128)}) %reduce-scatter.13.cloned.1.call-update) | async-done | bytes 1048592 | tf_op jit(solution)/shard_map/reduce_scatter | solution.py:215
  1269.6 78.0 %reduce-scatter.11.cloned.1.call-done = f32[128,2048]{1,0:T(8,128)} async-done(((f32[512,2048]{1,0:T(8,128)}), f32[128,2048]{1,0:T(8,128)}) %reduce-scatter.11.cloned.1.call-update) | async-done | bytes 1048592 | tf_op jit(solution)/shard_map/reduce_scatter | solution.py:186
  1350.6 32.8 %reduce-scatter.21.cloned.1.call-done = f32[128,16]{0,1:T(8,128)} async-done(((f32[1024,16]{0,1:T(8,128)}), f32[128,16]{0,1:T(8,128)}) %reduce-scatter.21.cloned.1.call-update) | async-done | bytes 8208 | tf_op jit(solution)/shard_map/reduce_scatter | solution.py:227
  1383.4 37.7 %reduce-scatter.19.cloned.1.call-done = f32[128,128]{1,0:T(8,128)} async-done(((f32[1024,128]{1,0:T(8,128)}), f32[128,128]{1,0:T(8,128)}) %reduce-scatter.19.cloned.1.call-update) | async-done | bytes 65552 | tf_op jit(solution)/shard_map/reduce_scatter | solution.py:225
  1421.0 38.6 %reduce-scatter.17.cloned.1.call-done = f32[128,160]{0,1:T(8,128)} async-done(((f32[1024,160]{0,1:T(8,128)}), f32[128,160]{0,1:T(8,128)}) %reduce-scatter.17.cloned.1.call-update) | async-done | bytes 81936 | tf_op jit(solution)/shard_map/reduce_scatter | solution.py:224
  1459.6 75.6 %reduce-scatter.23.cloned.1.call-done = f32[128,2048]{1,0:T(8,128)} async-done(((f32[1024,2048]{1,0:T(8,128)}), f32[128,2048]{1,0:T(8,128)}) %reduce-scatter.23.cloned.1.call-update) | async-done | bytes 1048592 | tf_op jit(solution)/shard_map/reduce_scatter | solution.py:229
  1535.2 120.1 %reduce-scatter.15.cloned.1.call-done = f32[2,128,2048]{2,1,0:T(8,128)} async-done(((f32[2,1024,2048]{2,1,0:T(8,128)}), f32[2,128,2048]{2,1,0:T(8,128)}) %reduce-scatter.15.cloned.1.call-update) | async-done | bytes 2097168 | tf_op jit(solution)/shard_map/reduce_scatter | solution.py:221
  (1076 shorter events, 955.0 us)
Async XLA Ops:
  7.2 60.5 %all-gather.9.cloned.1.call-start = ((), (), s32[]{:S(2)}) async-start(), calls=%async_computation.8 | async-start | bytes 2621440 | tf_op jit(solution)/shard_map/all_gather | solution.py:137
  7.9 105.5 %all-gather.11.cloned.1.call-start = ((), (), s32[]{:S(2)}) async-start(), calls=%async_computation.9 | async-start | bytes 9437184 | tf_op jit(solution)/shard_map/all_gather | solution.py:122
  8.7 152.3 %all-gather.15.cloned.1.call-start = ((), (), s32[]{:S(2)}) async-start(), calls=%async_computation.13 | async-start | bytes 2621440 | tf_op jit(solution)/shard_map/all_gather | solution.py:193
  9.4 188.8 %all-gather.13.cloned.1.call-start = ((), (), s32[]{:S(2)}) async-start(), calls=%async_computation.11 | async-start | bytes 4718592 | tf_op jit(solution)/shard_map/all_gather | solution.py:130
  10.0 238.8 %all-reduce.69.cloned.1.call-start = ((), (), s32[]{:S(2)}) async-start(), calls=%async_computation.10 | async-start | bytes 655360 | tf_op jit(solution)/shard_map/psum | solution.py:158
  67.5 143.2 %copy-start.83 = (bf16[1024,160]{0,1:T(8,128)(2,1)}, bf16[1024,160]{0,1:T(8,128)(2,1)S(1)}, u32[]{:S(2)}) copy-start(bf16[1024,160]{0,1:T(8,128)(2,1)S(1)} %all_gather.45) | copy-start | bytes 983044
  67.5 130.6 %copy-start.115 = (f32[512]{0:T(512)}, f32[512]{0:T(512)S(1)}, u32[]{:S(2)}) copy-start(f32[512]{0:T(512)S(1)} %get-tuple-element.1111) | copy-start | bytes 6148
  67.6 130.6 %copy-start.116 = (f32[512]{0:T(512)}, f32[512]{0:T(512)S(1)}, u32[]{:S(2)}) copy-start(f32[512]{0:T(512)S(1)} %get-tuple-element.1112) | copy-start | bytes 6148
  67.6 130.6 %copy-start.117 = (f32[512]{0:T(512)}, f32[512]{0:T(512)S(1)}, u32[]{:S(2)}) copy-start(f32[512]{0:T(512)S(1)} %get-tuple-element.1113) | copy-start | bytes 6148
  67.6 130.6 %copy-start.107 = (f32[1024,1]{0,1:T(1,128)}, f32[1024,1]{0,1:T(1,128)S(1)}, u32[]{:S(2)}) copy-start(f32[1024,1]{0,1:T(1,128)S(1)} %get-tuple-element.1108) | copy-start | bytes 12292
  67.6 130.6 %copy-start.109 = (f32[1024,1]{0,1:T(1,128)}, f32[1024,1]{0,1:T(1,128)S(1)}, u32[]{:S(2)}) copy-start(f32[1024,1]{0,1:T(1,128)S(1)} %get-tuple-element.1110) | copy-start | bytes 12292
  67.6 130.6 %copy-start.111 = (f32[1024,1]{0,1:T(1,128)}, f32[1024,1]{0,1:T(1,128)S(1)}, u32[]{:S(2)}) copy-start(f32[1024,1]{0,1:T(1,128)S(1)} %get-tuple-element.1109) | copy-start | bytes 12292
  67.6 130.6 %copy-start.113 = (f32[1024,1]{0,1:T(1,128)}, f32[1024,1]{0,1:T(1,128)S(1)}, u32[]{:S(2)}) copy-start(f32[1024,1]{0,1:T(1,128)S(1)} %get-tuple-element.1107) | copy-start | bytes 12292
  121.3 89.4 %copy-start.75 = (f32[509,1024]{1,0:T(8,128)}, f32[509,1024]{1,0:T(8,128)S(1)}, u32[]{:S(2)}) copy-start(f32[509,1024]{1,0:T(8,128)S(1)} %slice_bitcast_fusion.1) | copy-start | bytes 6254596
  212.0 1023.5 %reduce-scatter.25.cloned.1.call-start = ((), (), s32[]{:S(2)}) async-start(), calls=%async_computation.20 | async-start | bytes 589824
  255.4 246.5 %copy-start.81 = (f32[1024,16]{0,1:T(8,128)S(1)}, f32[1024,16]{0,1:T(8,128)}, u32[]{:S(2)}) copy-start(f32[1024,16]{0,1:T(8,128)} %get-tuple-element.1815) | copy-start | bytes 196612
  1156.8 111.3 %reduce-scatter.13.cloned.1.call-start = ((), (), s32[]{:S(2)}) async-start(), calls=%async_computation.14 | async-start | bytes 5242880 | tf_op jit(solution)/shard_map/reduce_scatter | solution.py:215
  1168.1 179.4 %reduce-scatter.11.cloned.1.call-start = ((), (), s32[]{:S(2)}) async-start(), calls=%async_computation.12 | async-start | bytes 5242880 | tf_op jit(solution)/shard_map/reduce_scatter | solution.py:186
  1175.0 208.3 %reduce-scatter.21.cloned.1.call-start = ((), (), s32[]{:S(2)}) async-start(), calls=%async_computation.18 | async-start | bytes 73728 | tf_op jit(solution)/shard_map/reduce_scatter | solution.py:227
  1175.8 245.2 %reduce-scatter.19.cloned.1.call-start = ((), (), s32[]{:S(2)}) async-start(), calls=%async_computation.17 | async-start | bytes 589824 | tf_op jit(solution)/shard_map/reduce_scatter | solution.py:225
  1177.2 282.5 %reduce-scatter.17.cloned.1.call-start = ((), (), s32[]{:S(2)}) async-start(), calls=%async_computation.16 | async-start | bytes 737280 | tf_op jit(solution)/shard_map/reduce_scatter | solution.py:224
  1178.6 356.6 %reduce-scatter.23.cloned.1.call-start = ((), (), s32[]{:S(2)}) async-start(), calls=%async_computation.19 | async-start | bytes 9437184 | tf_op jit(solution)/shard_map/reduce_scatter | solution.py:229
  1186.5 468.9 %reduce-scatter.15.cloned.1.call-start = ((), (), s32[]{:S(2)}) async-start(), calls=%async_computation.15 | async-start | bytes 18874368 | tf_op jit(solution)/shard_map/reduce_scatter | solution.py:221
  1196.0 151.5 %copy-start.88 = (bf16[128,2048]{1,0:T(8,128)(2,1)S(1)}, bf16[128,2048]{1,0:T(8,128)(2,1)}, u32[]{:S(2)}) copy-start(bf16[128,2048]{1,0:T(8,128)(2,1)} %param.25) | copy-start | bytes 1572868
  (229 other events, 3635.3 us)
Sparse Core Ops, SparseCore 0:
  9.6 48.7 all-gather.8
  60.3 53.0 all-gather.10
  115.0 45.9 all-gather.14
  162.7 35.4 all-gather.12
  212.1 36.2 all-reduce.68
  1156.9 31.4 reduce-scatter.24
  1190.8 77.2 reduce-scatter.12
  1270.3 77.1 reduce-scatter.10
  1351.4 31.9 reduce-scatter.20
  1386.9 34.1 reduce-scatter.18
  1425.0 34.5 reduce-scatter.16
  1463.9 71.2 reduce-scatter.22
  1539.4 115.9 reduce-scatter.14
where the time goes:
time: 1680 us; the launch traced here: 1660 us
  other arithmetic  657 us (39%)
  waiting for transfers between devices  533 us (32%)
  local copies, waits for them, and re-layouts  187 us (11%)
  blocking collectives  147 us (9%)
  matrix products  71.2 us (4%)
  loops' own time  48.6 us (3%)
  between operations  17.3 us (1%)
    while x86, other arithmetic  135 us
    reduce_scatter x1, waiting for transfers between devices, shards(): lax.psum_scatter(w_in_grad, 'fsdp', scatter_dimension=1, tiled=True)  120 us
    while x432, local copies, waits for them, and re-layouts  96.3 us
    mul x20, other arithmetic, block_scan(): product = factors[:, offset] * product  84 us
    reduce_scatter x1, waiting for transfers between devices, shards(): lax.psum_scatter(jnp.dot(gated_low, w_out_t, preferred_element_type=f32),...  78 us
    reduce_scatter x1, waiting for transfers between devices, shards(): lax.psum_scatter(out_grad, 'fsdp', scatter_dimension=0, tiled=True)  75.6 us
    add x64, other arithmetic, carry_step(): return (members[0] * current + members[1], current)  57.8 us
    mul x28, other arithmetic, block_scan(): running = factors[:, offset] * running + drives[:, offset]  55.4 us
  transfers between devices with their start and end apart: 13, of which 10 were waited for; matrix products, arithmetic and copies ran while one was open for 4% of the time, Pallas kernels for 0%

commit v1 on v0

--- a/solution.py
+++ b/solution.py
@@ -190,7 +190,8 @@
         tiled=True,
     )
     output = (hidden.astype(f32) + branch).astype(bf16)
-    cot_all = lax.all_gather(cotangent, "tensor", axis=0, tiled=True)
+    sent = jnp.stack([cotangent] * lax.axis_size("tensor"))
+    cot_all = jnp.concatenate(lax.all_to_all(sent, "tensor", 0, 0), axis=0)
     grad_gated = (
         jnp.einsum("gd,cd->gc", cot_all, w_out_t, preferred_element_type=f32)
         .astype(bf16)

time: 1680 us -> 1670 us (level)
  waiting for transfers between devices: 533 us -> 460 us
  blocking collectives: 147 us -> 205 us
    all_gather x1, blocking collectives: 12.4 us -> 69.2 us  [shards(): lax.all_gather(gain_fsdp, 'tensor', axis=0, tiled=True)]
    all_gather x1 -> x0, waiting for transfers between devices: 35.7 us -> none  [shards(): cot_all = lax.all_gather(cotangent, 'tensor', axis=0, tiled=True)]
    all_gather x1, waiting for transfers between devices: 43.4 us -> 18 us  [shards(): lax.all_gather(w_in, 'fsdp', axis=1, tiled=True)]
  transfers between devices with their start and end apart: 13 -> 13, of which waited for: 10 -> 9; matrix products, arithmetic and copies ran while one was open for 4% -> 4% of each run, Pallas kernels for 0% -> 0%
where the time goes in v1:
time: 1670 us; the launch traced here: 1660 us
  other arithmetic  657 us (39%)
  waiting for transfers between devices  460 us (28%)
  blocking collectives  205 us (12%)
  local copies, waits for them, and re-layouts  190 us (11%)
  matrix products  71.3 us (4%)
  loops' own time  48.6 us (3%)
  between operations  17.6 us (1%)
    while x86, other arithmetic  135 us
    reduce_scatter x1, waiting for transfers between devices, shards(): lax.psum_scatter(w_in_grad, 'fsdp', scatter_dimension=1, tiled=True)  120 us
    while x432, local copies, waits for them, and re-layouts  96.3 us
    mul x20, other arithmetic, block_scan(): product = factors[:, offset] * product  84 us
    reduce_scatter x1, waiting for transfers between devices, shards(): lax.psum_scatter(jnp.dot(gated_low, w_out_t, preferred_element_type=f32),...  77.8 us
    reduce_scatter x1, waiting for transfers between devices, shards(): lax.psum_scatter(out_grad, 'fsdp', scatter_dimension=0, tiled=True)  75.8 us
    all_gather x1, blocking collectives, shards(): lax.all_gather(gain_fsdp, 'tensor', axis=0, tiled=True)  69.2 us
    add x64, other arithmetic, carry_step(): return (members[0] * current + members[1], current)  57.8 us
  transfers between devices with their start and end apart: 13, of which 9 were waited for; matrix products, arithmetic and copies ran while one was open for 4% of the time, Pallas kernels for 0%

profile of v1, /device:TPU:0, one launch (start us, length us, event | category | flops | bytes accessed | tf_op | source)
XLA Modules:
  0.0 1656.3 jit_solution(11614225083900799068)
XLA Ops:
  36.4 69.2 %all-gather.1 = bf16[4,1,512]{2,1,0:T(2,128)(2,1)S(1)} all-gather(bf16[1,1,512]{2,1,0:T(2,128)(2,1)S(1)} %reshape.412), channel_id=1, replica_groups=mesh['fsdp'=8,'tensor'=4] {'tensor'}, dimensions={0}, use_global_device_ids=true | all-gather | bytes 5120 | tf_op jit(solution)/shard_map/all_gather | solution.py:138
  135.7 18.0 %all-gather.10.cloned.1.call-done = bf16[2,1024,2048]{2,1,0:T(8,128)(2,1)} async-done(((bf16[2,128,2048]{2,1,0:T(8,128)(2,1)}), bf16[2,1024,2048]{2,1,0:T(8,128)(2,1)}) %all-gather.10.cloned.1.call-update) | async-done | bytes 8388624 | tf_op jit(solution)/shard_map/all_gather | solution.py:122
  165.5 25.9 %all-gather.12.cloned.1.call-done = bf16[1024,2048]{1,0:T(8,128)(2,1)} async-done(((bf16[128,2048]{1,0:T(8,128)(2,1)}), bf16[1024,2048]{1,0:T(8,128)(2,1)}) %all-gather.12.cloned.1.call-update) | async-done | bytes 4194320 | tf_op jit(solution)/shard_map/all_gather | solution.py:130
  248.7 242.5 %while.116 = (s32[]{:T(128)}, f32[1024,16]{0,1:T(8,128)S(1)}, f32[2,256,1024]{2,1,0:T(8,128)}, f32[2,1024,16]{1,2,0:T(8,128)}, f32[2,256,1024]{2,1,0:T(8,128)}, ...) while((s32[]{:T(128)}, f32[1024,16]{0,1:T(8,128)S(1)}, ...), condition=%wide.region_9.10_spmd, body=%wide.region_5.9_spmd.sunk | while | flops 52199424 | bytes 568369280 | solution.py:83
  336.1 24.8 %while.120 = (s32[]{:T(128)}, f32[1024,16]{0,1:T(8,128)S(1)}, f32[16,1024,16]{1,2,0:T(8,128)}, f32[16,1024,16]{1,2,0:T(8,128)}, f32[16,1024,16]{1,2,0:T(8,128)}, /*index=5*/s32[]{:T(128)}) while((s32[]{:T(128)}, f32[1024,16]{0,1:T(8,128)S(1)}, f32[16,1024,16]{1,2,0:T(8,128)}, f32[16,1024,16]{1,2,0:T(8,128)}, f32[16,1024,16]{1,2,0:T(8,128)}, ...), condition=%wide.region_7.7_spmd, body=%wide.region_6.6_spmd.sunk | while | flops 32770 | bytes 393801 | solution.py:62
  450.5 24.8 %while.120 = (s32[]{:T(128)}, f32[1024,16]{0,1:T(8,128)S(1)}, f32[16,1024,16]{1,2,0:T(8,128)}, f32[16,1024,16]{1,2,0:T(8,128)}, f32[16,1024,16]{1,2,0:T(8,128)}, /*index=5*/s32[]{:T(128)}) while((s32[]{:T(128)}, f32[1024,16]{0,1:T(8,128)S(1)}, f32[16,1024,16]{1,2,0:T(8,128)}, f32[16,1024,16]{1,2,0:T(8,128)}, f32[16,1024,16]{1,2,0:T(8,128)}, ...), condition=%wide.region_7.7_spmd, body=%wide.region_6.6_spmd.sunk | while | flops 32770 | bytes 393801 | solution.py:62
  495.6 609.4 %while.119 = (s32[]{:T(128)}, f32[1024,16]{0,1:T(8,128)}, f32[1024,16]{0,1:T(8,128)S(1)}, f32[2,256,1024]{2,1,0:T(8,128)}, f32[2,256,1024]{2,1,0:T(8,128)}, /*in...) while((s32[]{:T(128)}, f32[1024,16]{0,1:T(8,128)}, ...), condition=%wide.region_22.23_spmd.clone, body=%wide.region_11.22_spmd.clone.sunk | while | flops 338518016 | bytes 1045472448 | solution.py:83
  628.2 15.0 while.121
  659.8 24.9 %while.122 = (s32[]{:T(128)}, f32[1024,16]{0,1:T(8,128)S(1)}, f32[16,1024,16]{1,2,0:T(8,128)S(1)}, f32[16,1024,16]{1,2,0:T(8,128)}, f32[16,1024,16]{1,2,0:T(8,12...) while((s32[]{:T(128)}, f32[1024,16]{0,1:T(8,128)S(1)}, ...), condition=%wide.region_16.16_spmd, body=%wide.region_15.15_spmd.sunk | while | flops 49155 | bytes 524401 | solution.py:62
  699.5 15.5 slice_add_fusion.81
  787.6 14.9 multiply_reduce_fusion.17
  917.5 15.0 while.121
  949.1 24.9 %while.122 = (s32[]{:T(128)}, f32[1024,16]{0,1:T(8,128)S(1)}, f32[16,1024,16]{1,2,0:T(8,128)S(1)}, f32[16,1024,16]{1,2,0:T(8,128)}, f32[16,1024,16]{1,2,0:T(8,12...) while((s32[]{:T(128)}, f32[1024,16]{0,1:T(8,128)S(1)}, ...), condition=%wide.region_16.16_spmd, body=%wide.region_15.15_spmd.sunk | while | flops 49155 | bytes 524401 | solution.py:62
  988.8 15.5 slice_add_fusion.81
  1076.9 14.9 multiply_reduce_fusion.17
  1112.1 25.8 %all-reduce.70 = bf16[512,160]{0,1:T(8,128)(2,1)S(1)} all-reduce(f32[512,160]{0,1:T(8,128)S(1)} %pad_maximum_fusion.3), channel_id=1, replica_groups=mesh['fsdp'=8,'tensor'=4] {'tensor'}, use_global_device_ids=true, to_apply=%region_23.24 | all-reduce | flops 81920 | bytes 491520 | tf_op jit(solution)/shard_map/psum | solution.py:205
  1203.1 23.9 %all-reduce.65 = (f32[512]{0:T(512)S(1)}, f32[1024]{0:T(1024)S(1)}, f32[1024]{0:T(1024)S(1)}, f32[1024]{0:T(1024)S(1)}) all-reduce(f32[512]{0:T(512)S(1)} %dynamic-slice.2, f32[1024]{0:T(1024)S(1)} %get-tuple-element.866, f32[1024]{0:T(1024)S(1)} %get-tuple-element.1057, ...), channel_id=5, replica_groups=mesh['fsdp'=8,'tensor'=4] {'fsdp'}, use_global_device_ids=true, to_apply=%region_29.30.clone | all-reduce | flops 3584 | bytes 28672
  1230.9 31.1 %reduce-scatter.13.cloned.1.call-done = f32[128,2048]{1,0:T(8,128)} async-done(((f32[512,2048]{1,0:T(8,128)}), f32[128,2048]{1,0:T(8,128)}) %reduce-scatter.13.cloned.1.call-update) | async-done | bytes 1048592 | tf_op jit(solution)/shard_map/reduce_scatter | solution.py:216
  1263.6 77.8 %reduce-scatter.11.cloned.1.call-done = f32[128,2048]{1,0:T(8,128)} async-done(((f32[512,2048]{1,0:T(8,128)}), f32[128,2048]{1,0:T(8,128)}) %reduce-scatter.11.cloned.1.call-update) | async-done | bytes 1048592 | tf_op jit(solution)/shard_map/reduce_scatter | solution.py:186
  1344.5 32.7 %reduce-scatter.21.cloned.1.call-done = f32[128,16]{0,1:T(8,128)} async-done(((f32[1024,16]{0,1:T(8,128)}), f32[128,16]{0,1:T(8,128)}) %reduce-scatter.21.cloned.1.call-update) | async-done | bytes 8208 | tf_op jit(solution)/shard_map/reduce_scatter | solution.py:228
  1377.2 37.8 %reduce-scatter.19.cloned.1.call-done = f32[128,128]{1,0:T(8,128)} async-done(((f32[1024,128]{1,0:T(8,128)}), f32[128,128]{1,0:T(8,128)}) %reduce-scatter.19.cloned.1.call-update) | async-done | bytes 65552 | tf_op jit(solution)/shard_map/reduce_scatter | solution.py:226
  1415.0 38.4 %reduce-scatter.17.cloned.1.call-done = f32[128,160]{0,1:T(8,128)} async-done(((f32[1024,160]{0,1:T(8,128)}), f32[128,160]{0,1:T(8,128)}) %reduce-scatter.17.cloned.1.call-update) | async-done | bytes 81936 | tf_op jit(solution)/shard_map/reduce_scatter | solution.py:225
  1453.5 75.8 %reduce-scatter.23.cloned.1.call-done = f32[128,2048]{1,0:T(8,128)} async-done(((f32[1024,2048]{1,0:T(8,128)}), f32[128,2048]{1,0:T(8,128)}) %reduce-scatter.23.cloned.1.call-update) | async-done | bytes 1048592 | tf_op jit(solution)/shard_map/reduce_scatter | solution.py:230
  1529.2 120.0 %reduce-scatter.15.cloned.1.call-done = f32[2,128,2048]{2,1,0:T(8,128)} async-done(((f32[2,1024,2048]{2,1,0:T(8,128)}), f32[2,128,2048]{2,1,0:T(8,128)}) %reduce-scatter.15.cloned.1.call-update) | async-done | bytes 2097168 | tf_op jit(solution)/shard_map/reduce_scatter | solution.py:222
  (1076 shorter events, 952.8 us)
Async XLA Ops:
  7.2 126.4 %all-gather.8.cloned.1.call-start = ((), (), s32[]{:S(2)}) async-start(), calls=%async_computation.9 | async-start | bytes 2621440 | tf_op jit(solution)/shard_map/all_gather | solution.py:137
  7.9 145.8 %all-gather.10.cloned.1.call-start = ((), (), s32[]{:S(2)}) async-start(), calls=%async_computation.10 | async-start | bytes 9437184 | tf_op jit(solution)/shard_map/all_gather | solution.py:122
  8.7 182.7 %all-gather.12.cloned.1.call-start = ((), (), s32[]{:S(2)}) async-start(), calls=%async_computation.12 | async-start | bytes 4718592 | tf_op jit(solution)/shard_map/all_gather | solution.py:130
  12.0 153.5 %all-to-all-start = ((bf16[4,128,2048]{2,1,0:T(8,128)(2,1)}), bf16[4,128,2048]{2,1,0:T(8,128)(2,1)}, u32[]{:S(2)}, u32[]{:S(2)}) async-start(bf16[4,128,2048]{2,1,0:T(8,128)(2,1)} %stack.65), calls=%async_computation.1 | async-start | bytes 4194304 | tf_op jit(solution)/shard_map/all_to_all | solution.py:194
  18.3 223.7 %all-reduce.69.cloned.1.call-start = ((), (), s32[]{:S(2)}) async-start(), calls=%async_computation.11 | async-start | bytes 655360 | tf_op jit(solution)/shard_map/psum | solution.py:158
  133.4 70.5 %copy-start.83 = (bf16[1024,160]{0,1:T(8,128)(2,1)}, bf16[1024,160]{0,1:T(8,128)(2,1)S(1)}, u32[]{:S(2)}) copy-start(bf16[1024,160]{0,1:T(8,128)(2,1)S(1)} %all_gather.42) | copy-start | bytes 983044
  133.4 58.0 %copy-start.115 = (f32[512]{0:T(512)}, f32[512]{0:T(512)S(1)}, u32[]{:S(2)}) copy-start(f32[512]{0:T(512)S(1)} %get-tuple-element.1111) | copy-start | bytes 6148
  133.4 58.0 %copy-start.116 = (f32[512]{0:T(512)}, f32[512]{0:T(512)S(1)}, u32[]{:S(2)}) copy-start(f32[512]{0:T(512)S(1)} %get-tuple-element.1112) | copy-start | bytes 6148
  133.4 58.0 %copy-start.117 = (f32[512]{0:T(512)}, f32[512]{0:T(512)S(1)}, u32[]{:S(2)}) copy-start(f32[512]{0:T(512)S(1)} %get-tuple-element.1113) | copy-start | bytes 6148
  133.5 57.9 %copy-start.107 = (f32[1024,1]{0,1:T(1,128)}, f32[1024,1]{0,1:T(1,128)S(1)}, u32[]{:S(2)}) copy-start(f32[1024,1]{0,1:T(1,128)S(1)} %get-tuple-element.1108) | copy-start | bytes 12292
  133.5 57.9 %copy-start.109 = (f32[1024,1]{0,1:T(1,128)}, f32[1024,1]{0,1:T(1,128)S(1)}, u32[]{:S(2)}) copy-start(f32[1024,1]{0,1:T(1,128)S(1)} %get-tuple-element.1110) | copy-start | bytes 12292
  133.5 57.9 %copy-start.111 = (f32[1024,1]{0,1:T(1,128)}, f32[1024,1]{0,1:T(1,128)S(1)}, u32[]{:S(2)}) copy-start(f32[1024,1]{0,1:T(1,128)S(1)} %get-tuple-element.1109) | copy-start | bytes 12292
  133.5 57.9 %copy-start.113 = (f32[1024,1]{0,1:T(1,128)}, f32[1024,1]{0,1:T(1,128)S(1)}, u32[]{:S(2)}) copy-start(f32[1024,1]{0,1:T(1,128)S(1)} %get-tuple-element.1107) | copy-start | bytes 12292
  205.2 1024.2 %reduce-scatter.25.cloned.1.call-start = ((), (), s32[]{:S(2)}) async-start(), calls=%async_computation.20 | async-start | bytes 589824
  248.7 246.9 %copy-start.81 = (f32[1024,16]{0,1:T(8,128)S(1)}, f32[1024,16]{0,1:T(8,128)}, u32[]{:S(2)}) copy-start(f32[1024,16]{0,1:T(8,128)} %get-tuple-element.1815) | copy-start | bytes 196612
  1150.9 111.2 %reduce-scatter.13.cloned.1.call-start = ((), (), s32[]{:S(2)}) async-start(), calls=%async_computation.14 | async-start | bytes 5242880 | tf_op jit(solution)/shard_map/reduce_scatter | solution.py:216
  1162.2 179.2 %reduce-scatter.11.cloned.1.call-start = ((), (), s32[]{:S(2)}) async-start(), calls=%async_computation.13 | async-start | bytes 5242880 | tf_op jit(solution)/shard_map/reduce_scatter | solution.py:186
  1169.2 208.1 %reduce-scatter.21.cloned.1.call-start = ((), (), s32[]{:S(2)}) async-start(), calls=%async_computation.18 | async-start | bytes 73728 | tf_op jit(solution)/shard_map/reduce_scatter | solution.py:228
  1169.9 245.1 %reduce-scatter.19.cloned.1.call-start = ((), (), s32[]{:S(2)}) async-start(), calls=%async_computation.17 | async-start | bytes 589824 | tf_op jit(solution)/shard_map/reduce_scatter | solution.py:226
  1171.3 282.2 %reduce-scatter.17.cloned.1.call-start = ((), (), s32[]{:S(2)}) async-start(), calls=%async_computation.16 | async-start | bytes 737280 | tf_op jit(solution)/shard_map/reduce_scatter | solution.py:225
  1172.8 356.5 %reduce-scatter.23.cloned.1.call-start = ((), (), s32[]{:S(2)}) async-start(), calls=%async_computation.19 | async-start | bytes 9437184 | tf_op jit(solution)/shard_map/reduce_scatter | solution.py:230
  1180.6 468.7 %reduce-scatter.15.cloned.1.call-start = ((), (), s32[]{:S(2)}) async-start(), calls=%async_computation.15 | async-start | bytes 18874368 | tf_op jit(solution)/shard_map/reduce_scatter | solution.py:222
  1190.3 71.7 %copy-start.82 = (bf16[128,2048]{1,0:T(8,128)(2,1)S(1)}, bf16[128,2048]{1,0:T(8,128)(2,1)}, u32[]{:S(2)}) copy-start(bf16[128,2048]{1,0:T(8,128)(2,1)} %param.24) | copy-start | bytes 1572868
  1190.3 151.1 %copy-start.88 = (bf16[128,2048]{1,0:T(8,128)(2,1)S(1)}, bf16[128,2048]{1,0:T(8,128)(2,1)}, u32[]{:S(2)}) copy-start(bf16[128,2048]{1,0:T(8,128)(2,1)} %param.25) | copy-start | bytes 1572868
  (229 other events, 3556.6 us)
Sparse Core Ops, SparseCore 0:
  9.6 86.4 all-gather.7
  98.0 55.6 all-gather.9
  155.6 35.7 all-gather.11
  205.3 36.2 all-reduce.68
  1151.0 31.4 reduce-scatter.24
  1184.7 77.2 reduce-scatter.12
  1264.3 77.0 reduce-scatter.10
  1345.3 31.9 reduce-scatter.20
  1380.9 34.1 reduce-scatter.18
  1418.9 34.5 reduce-scatter.16
  1457.9 71.2 reduce-scatter.22
  1533.2 115.9 reduce-scatter.14
